TPU v7x, 512 devices: a whole 4x4x16 slice. The times are simulated.
512 devices in a mesh: seq: 64 (over z, x_hi, core), head: 8 (over x_lo, y).
Axes of the slice: x: 4 (x_hi: 2, x_lo: 2; x = x_hi * 2 + x_lo), y: 4, z: 16, core: 2. Of those that a mesh axis runs over, the one named last changes fastest.
Arguments:
- attention: bfloat16 [16, 4096, 1536], P(None, 'seq', 'head'), may hold values from -6 to 6
- encoder_skip: bfloat16 [16, 8192, 1536], P('head', 'seq'), may hold values from -6 to 6
- depth_filter: float32 [3, 1536], replicated, may hold values from -3 to 3
- point_weight: bfloat16 [1536, 1536], P('head'), may hold values from -0.15625 to 0.15625
- crop_offset: int32 [16], P('head'), may hold values from 0 to 128
- target_bins: int32 [16, 128], P('head'), may hold values from 0 to 127
- cotangent: bfloat16 [16, 8192, 1536], P('head', 'seq'), may hold values from -6 to 6
Outputs:
- target_rows: bfloat16 [16, 128, 1536], P('head', 'seq')
- attention_grad: bfloat16 [16, 4096, 1536], P('head', 'seq')
- skip_grad: bfloat16 [16, 8192, 1536], P('head', 'seq')
- filter_grad: float32 [3, 1536], replicated
Inputs may be any that keep to these rules, and one draw needn't show every extreme that they name: The cropped window of sequence b starts at bin crop_offset[b]; bins of it past the end of the sequence are empty. Target j of sequence b reads bin 128 * (j // 2) + target_bins[b, j] of the cropped window.
All inputs are finite; a program needn't handle non-finite values.
Results may differ from a plain program's by a relative error of at most 0.007.
Values may be sent and summed in bfloat16 or wider, within the bound.
A program may use at most 64 MiB of HBM per device.

v0:
```python
import math
import jax
import jax.numpy as jnp
from jax import lax
from jax.sharding import PartitionSpec as P

NTD = 2


def extended(shard, sides, width):
    for axis, dim in sides:
        count, length = (lax.axis_size(axis), shard.shape[dim])
        up = [(i, (i + 1) % count) for i in range(count - 1)]
        down = [(j, i) for i, j in up]
        last = lax.slice_in_dim(shard, length - width, length, axis=dim)
        initial = lax.slice_in_dim(shard, 0, width, axis=dim)
        before = lax.ppermute(last, axis, up)
        after = lax.ppermute(initial, axis, down)
        shard = jnp.concatenate([before, shard, after], axis=dim)
    return shard


def passed_along(shard, axis, by):
    count = lax.axis_size(axis)
    pairs = [(i, i + by) for i in range(count) if 0 <= i + by < count]
    return lax.ppermute(shard, axis, pairs)


def gelu_slope(values):
    return (
        0.5 * (1.0 + lax.erf(values * 0.7071067811865476))
        + values * jnp.exp(-0.5 * values * values) * 0.3989422804014327
    )


def with_rims(field):
    return extended(field, (("seq", 1),), 1)


def one_hot(places, length):
    return (places[:, :, None] == jnp.arange(length, dtype=jnp.int32)[None, None, :]).astype(
        jnp.bfloat16
    )


def shards(
    attention, encoder_skip, depth_filter, point_weight, crop_offset, target_bins, cotangent
):
    slab_input = lax.all_to_all(attention, "head", split_axis=0, concat_axis=2, tiled=True)
    local_seqs = encoder_skip.shape[0]
    slab_rows = encoder_skip.shape[1]
    channels = encoder_skip.shape[2]
    summed = (
        jnp.repeat(slab_input, 2, axis=1).astype(jnp.float32) + encoder_skip.astype(jnp.float32)
    ).astype(jnp.bfloat16)
    padded = with_rims(summed)
    filtered = (
        depth_filter[0] * padded[:, :-2]
        + depth_filter[1] * padded[:, 1:-1]
        + depth_filter[2] * padded[:, 2:]
    )
    activated = jax.nn.gelu(filtered, approximate=False).astype(jnp.bfloat16)
    flat_act = activated.reshape(local_seqs * slab_rows, channels)
    full_weight = lax.all_gather(point_weight, "head", axis=0, tiled=True)
    mixed_rows = jnp.dot(flat_act, full_weight, preferred_element_type=jnp.float32)
    block_out = (
        summed.astype(jnp.float32) + mixed_rows.reshape(local_seqs, slab_rows, channels)
    ).astype(jnp.bfloat16)
    slab_index = lax.axis_index("seq")
    my_places = (
        lax.dynamic_slice_in_dim(target_bins, slab_index * NTD, NTD, 1) + crop_offset[:, None]
    )
    next_block = passed_along(block_out, "seq", -1)
    joined = jnp.concatenate([block_out, next_block], axis=1)
    target_rows = jnp.einsum(
        "sjr,srd->sjd",
        one_hot(my_places, 2 * slab_rows),
        joined,
        preferred_element_type=jnp.float32,
    ).astype(jnp.bfloat16)
    prev_cot = passed_along(cotangent, "seq", 1)
    cot_pair = jnp.concatenate([prev_cot, cotangent], axis=1)

    def crop_back(cot_block, shift_by):
        return lax.dynamic_slice_in_dim(cot_block, slab_rows - shift_by, slab_rows, 0)

    grad_out = jax.vmap(crop_back)(cot_pair, crop_offset)
    flat_grad = grad_out.reshape(local_seqs * slab_rows, channels)
    grad_act = lax.dot_general(
        flat_grad, full_weight, (((1,), (1,)), ((), ())), preferred_element_type=jnp.float32
    )
    grad_conv = (grad_act.reshape(local_seqs, slab_rows, channels) * gelu_slope(filtered)).astype(
        jnp.bfloat16
    )
    grad_padded = with_rims(grad_conv)
    grad_sum = (
        grad_out.astype(jnp.float32)
        + depth_filter[0] * grad_padded[:, 2:]
        + depth_filter[1] * grad_padded[:, 1:-1]
        + depth_filter[2] * grad_padded[:, :-2]
    )
    skip_grad = grad_sum.astype(jnp.bfloat16)
    attention_grad = (
        grad_sum.reshape(local_seqs, slab_rows // 2, 2, channels).sum(axis=2).astype(jnp.bfloat16)
    )
    filter_terms = jnp.stack(
        [
            jnp.einsum(
                "srd,srd->d", grad_conv, padded[:, 0:slab_rows], preferred_element_type=jnp.float32
            ),
            jnp.einsum(
                "srd,srd->d",
                grad_conv,
                padded[:, 1 : slab_rows + 1],
                preferred_element_type=jnp.float32,
            ),
            jnp.einsum(
                "srd,srd->d",
                grad_conv,
                padded[:, 2 : slab_rows + 2],
                preferred_element_type=jnp.float32,
            ),
        ]
    )
    filter_sum = lax.psum(filter_terms, ("seq", "head"))
    row_count = local_seqs * lax.axis_size("head") * slab_rows * lax.axis_size("seq")
    filter_grad = filter_sum * (1.0 / math.sqrt(row_count))
    return (target_rows, attention_grad, skip_grad, filter_grad)


def solution(mesh):
    in_specs = (
        P(None, "seq", "head"),
        P("head", "seq", None),
        P(),
        P("head", None),
        P("head"),
        P("head", None),
        P("head", "seq", None),
    )
    out_specs = (P("head", "seq", None), P("head", "seq", None), P("head", "seq", None), P())
    return jax.shard_map(shards, mesh=mesh, in_specs=in_specs, out_specs=out_specs, check_vma=False)
```

profile of v0, /device:TPU:32, one launch (start us, length us, event | category | flops | bytes accessed | tf_op | source)
XLA Modules:
  0.0 226.0 jit_solution(16963135204489975365)
XLA Ops:
  7.2 0.0 copy-start.6
  7.2 0.0 copy-start.4
  7.2 0.0 copy-start.5
  7.2 0.0 all-gather.2.cloned.1.call-start
  7.2 0.7 all-gather.2.cloned.1.call-update
  7.9 5.4 %all-to-all-start = ((bf16[16,64,192]{2,1,0:T(8,128)(2,1)}), bf16[16,64,192]{2,1,0:T(8,128)(2,1)S(1)}, u32[]{:S(2)}, u32[]{:S(2)}) async-start(bf16[16,64,192]{2,1,0:T(8,128)(2,1)} %param.7), calls=%async_computation | async-start | bytes 1048576 | tf_op jit(solution)/shard_map/all_to_all | solution.py:49
  13.3 1.9 collective-permute-start.3
  15.3 0.0 copy-done.6
  15.3 0.1 copy.13
  15.4 0.0 copy-done.4
  15.4 0.1 slice_reduce_fusion.2
  15.5 0.0 copy-done.5
  15.5 0.1 dynamic-slice_add_fusion
  15.6 7.4 %all-to-all-done = bf16[16,64,192]{2,1,0:T(8,128)(2,1)S(1)} async-done(((bf16[16,64,192]{2,1,0:T(8,128)(2,1)}), bf16[16,64,192]{2,1,0:T(8,128)(2,1)S(1)}, u32[]{:S(2)}, u32[]{:S(2)}) %all-to-all-start) | async-done | bytes 393248 | tf_op jit(solution)/shard_map/all_to_all | solution.py:49
  22.9 0.3 copy.36
  23.2 0.3 reshape.54
  23.6 0.5 broadcast_in_dim.4
  24.1 1.1 convert_element_type.67
  25.2 1.3 add_convert_fusion
  26.5 0.0 copy-start
  26.6 1.9 collective-permute-start
  28.5 0.0 copy-start.2
  28.5 6.2 %collective-permute-start.1 = (bf16[2,1,1536]{2,1,0:T(2,128)(2,1)S(1)}, bf16[2,1,1536]{2,1,0:T(2,128)(2,1)S(1)}, u32[]{:S(2)}, u32[]{:S(2)}) collective-permute-start(bf16[2,1,1536]{2,1,0:T(2,128)(2,1)S(1)} %get-tuple-element.41), channel_id=1, source_target_pairs={{8,0},{16,8},{24,16},{32,24},{40,32},{48,40},{56,48},{64,56},{72,6... | collective-permute-start | bytes 18440 | tf_op jit(solution)/shard_map/ppermute | solution.py:18
  34.7 0.0 copy-done
  34.7 0.0 collective-permute-done.3
  34.7 1.5 pad_maximum_fusion
  36.2 0.0 copy-done.2
  36.2 0.0 copy-start.1
  36.2 4.0 %while.1 = (s32[]{:T(128)}, bf16[2,256,1536]{2,1,0:T(8,128)(2,1)S(1)}, s32[2,3]{1,0:T(2,128)S(1)}, bf16[2,128,1536]{2,1,0:T(8,128)(2,1)S(1)}, s32[]{:T(128)}) while((s32[]{:T(128)}, bf16[2,256,1536]{2,1,0:T(8,128)(2,1)S(1)}, s32[2,3]{1,0:T(2,128)S(1)}, bf16[2,128,1536]{2,1,0:T(8,128)(2,1)S(1)}, s32[]{:T(128)}) %tuple.38), condition=%wide.while_cond, body=%wide.while_body.sunk | while | flops 2 | bytes 786557 | solution.py:85
  36.3 0.6 fusion.117
  36.8 1.4 dynamic-slice_dynamic-update-slice_fusion.2
  38.3 0.6 fusion.117
  38.9 1.4 dynamic-slice_dynamic-update-slice_fusion.2
  40.3 0.0 copy-start.3
  40.3 0.0 collective-permute-done
  40.3 0.6 collective-permute-done.1
  40.9 38.8 %all-gather.2.cloned.1.call-done = bf16[1536,1536]{1,0:T(8,128)(2,1)} async-done(((bf16[192,1536]{1,0:T(8,128)(2,1)}), bf16[1536,1536]{1,0:T(8,128)(2,1)}) %all-gather.2.cloned.1.call-update) | async-done | bytes 4718608 | tf_op jit(solution)/shard_map/all_gather | solution.py:64
  79.7 0.0 copy-done.1
  79.7 0.0 copy-start.7
  79.7 8.3 %fusion.10 = bf16[2,128,1536]{2,1,0:T(8,128)(2,1)} fusion(bf16[1536,1536]{1,0:T(8,128)(2,1)} %all-gather.2.cloned.1.call-done, bf16[2,128,1536]{2,1,0:T(8,128)(2,1)S(1)} %copy-done.1, bf16[2,1,1536]{2,1,0:T(2,128)(2,1)S(1)} %collective-permute-done.1, bf16[2,1,1536]{2,1,0:T(2,128)(2,1)S(1)} %collective-permute-done, f32[1536]{0:T(1024)S(1)} %get-tuple-element.24, ...), kind=kOutput, calls=%fused_computation.8 | convolution fusion | flops 1240203264 | bytes 6322176 | tf_op jit(solution)/shard_map/dot_general | solution.py:65
  88.0 3.8 %collective-permute-start.2 = (bf16[2,128,1536]{2,1,0:T(8,128)(2,1)}, bf16[2,128,1536]{2,1,0:T(8,128)(2,1)}, u32[]{:S(2)}, u32[]{:S(2)}) collective-permute-start(bf16[2,128,1536]{2,1,0:T(8,128)(2,1)} %fusion.10), channel_id=1, source_target_pairs={{8,0},{16,8},{24,16},{32,24},{40,32},{48,40},{56,48},{64,56},{72,6... | collective-permute-start | bytes 2359304 | tf_op jit(solution)/shard_map/ppermute | solution.py:26
  91.8 0.0 copy-done.3
  91.8 0.0 copy-done.7
  91.8 2.9 %fusion.25 = (f32[1536]{0:T(1024)S(1)}, f32[1536]{0:T(1024)S(1)}, f32[1536]{0:T(1024)S(1)}, bf16[2,128,1536]{2,1,0:T(8,128)(2,1)S(1)}) fusion(bf16[2,128,1536]{2,1,0:T(8,128)(2,1)S(1)} %copy-done.1, bf16[2,1,1536]{2,1,0:T(2,128)(2,1)S(1)} %collective-permute-done, bf16[2,1,1536]{2,1,0:T(2,128)(2,1)S(1)} %collective-permute-done.1, ...), kind=kOutput, calls=%fused_computation.26 | convolution fusion | flops 1222110720 | bytes 7127040 | tf_op jit(solution)/shard_map/dot_general | solution.py:89
  94.8 105.9 %psum.7 = f32[3,1536]{1,0:T(4,128)S(1)} all-reduce(f32[3,1536]{1,0:T(4,128)S(1)} %pad_maximum_fusion.6), channel_id=1, replica_groups=mesh['seq'=64,'head'=8] {'seq','head'}, use_global_device_ids=true, to_apply=%region_1.0 | all-reduce | flops 4608 | bytes 36864 | tf_op jit(solution)/shard_map/psum | solution.py:125
  200.8 2.2 collective-permute-start.4
  203.0 2.3 %collective-permute-start.5 = (bf16[2,1,1536]{2,1,0:T(2,128)(2,1)S(1)}, bf16[2,1,1536]{2,1,0:T(2,128)(2,1)S(1)}, u32[]{:S(2)}, u32[]{:S(2)}) collective-permute-start(bf16[2,1,1536]{2,1,0:T(2,128)(2,1)S(1)} %get-tuple-element.39), channel_id=1, source_target_pairs={{0,8},{8,16},{16,24},{24,32},{32,40},{40,48},{48,56},{56,64},{64,7... | collective-permute-start | bytes 18440 | tf_op jit(solution)/shard_map/ppermute | solution.py:17
  205.3 0.6 broadcast_multiply_fusion
  205.9 0.0 collective-permute-done.4
  205.9 4.5 %collective-permute-done.5 = bf16[2,1,1536]{2,1,0:T(2,128)(2,1)S(1)} collective-permute-done((bf16[2,1,1536]{2,1,0:T(2,128)(2,1)S(1)}, bf16[2,1,1536]{2,1,0:T(2,128)(2,1)S(1)}, u32[]{:S(2)}, u32[]{:S(2)}) %collective-permute-start.5) | collective-permute-done | bytes 6176 | tf_op jit(solution)/shard_map/ppermute | solution.py:17
  210.4 2.7 %fusion.111 = (bf16[2,128,1536]{2,1,0:T(8,128)(2,1)}, f32[2,128,1536]{2,1,0:T(8,128)S(1)}) fusion(bf16[2,128,1536]{2,1,0:T(8,128)(2,1)S(1)} %get-tuple-element.42, bf16[2,1,1536]{2,1,0:T(2,128)(2,1)S(1)} %collective-permute-done.5, f32[1536]{0:T(1024)S(1)} %get-tuple-element.24, f32[1536]{0:T(1024)S(1)} %get-tuple-element.25, ...), kind=kLoop, calls=%fused_computation.134 | loop fusion | flops 6684672 | bytes 3962880 | tf_op jit(solution)/shard_map/convert_element_type | solution.py:102
  213.1 0.9 reshape.30
  214.0 2.8 %reduce_sum.9 = bf16[2,64,1536]{2,1,0:T(8,128)(2,1)} reduce(f32[2,64,2,1536]{3,2,1,0:T(2,128)S(1)} %reshape.30, f32[]{:T(128)} %constant.14.clone.1), dimensions={2}, to_apply=%region_0.0 | reduce | flops 196608 | bytes 1966084 | tf_op jit(solution)/shard_map/reduce_sum | solution.py:104
  216.8 0.0 collective-permute-done.2
  216.8 2.3 %convolution_convert_fusion = bf16[2,2,1536]{2,1,0:T(2,128)(2,1)} fusion(bf16[2,128,1536]{2,1,0:T(8,128)(2,1)} %collective-permute-done.2, bf16[2,128,1536]{2,1,0:T(8,128)(2,1)} %fusion.10, s32[2,2]{1,0:T(2,128)S(1)} %dynamic-slice_add_fusion), kind=kOutput, calls=%fused_computation.15 | convolution fusion | flops 6298624 | bytes 1585168 | tf_op jit(solution)/shard_map/sjr,srd->sjd/dot_general | solution.py:75
  (12 shorter events, 0.1 us)
Async XLA Ops:
  7.2 8.1 %copy-start.6 = (s32[2]{0:T(128)S(1)}, s32[2]{0:T(128)}, u32[]{:S(2)}) copy-start(s32[2]{0:T(128)} %param.11) | copy-start | bytes 28
  7.2 8.2 %copy-start.4 = (f32[3,1536]{1,0:T(4,128)S(1)}, f32[3,1536]{1,0:T(4,128)}, u32[]{:S(2)}) copy-start(f32[3,1536]{1,0:T(4,128)} %param.9) | copy-start | bytes 55300
  7.2 8.3 %copy-start.5 = (s32[2,128]{1,0:T(2,128)S(1)}, s32[2,128]{1,0:T(2,128)}, u32[]{:S(2)}) copy-start(s32[2,128]{1,0:T(2,128)} %param.12) | copy-start | bytes 3076
  7.2 72.5 %all-gather.2.cloned.1.call-start = ((), (), s32[]{:S(2)}) async-start(), calls=%async_computation.1 | async-start | bytes 5308416 | tf_op jit(solution)/shard_map/all_gather | solution.py:64
  7.9 15.0 %all-to-all-start = ((bf16[16,64,192]{2,1,0:T(8,128)(2,1)}), bf16[16,64,192]{2,1,0:T(8,128)(2,1)S(1)}, u32[]{:S(2)}, u32[]{:S(2)}) async-start(bf16[16,64,192]{2,1,0:T(8,128)(2,1)} %param.7), calls=%async_computation | async-start | bytes 1048576 | tf_op jit(solution)/shard_map/all_to_all | solution.py:49
  13.3 21.4 %collective-permute-start.3 = (bf16[2,128,1536]{2,1,0:T(8,128)(2,1)}, bf16[2,128,1536]{2,1,0:T(8,128)(2,1)}, u32[]{:S(2)}, u32[]{:S(2)}) collective-permute-start(bf16[2,128,1536]{2,1,0:T(8,128)(2,1)} %param.13), channel_id=1, source_target_pairs={{0,8},{8,16},{16,24},{24,32},{32,40},{40,48},{48,56},{56,64},{64,7... | collective-permute-start | bytes 2359304 | tf_op jit(solution)/shard_map/ppermute | solution.py:26
  26.5 8.2 %copy-start = (bf16[2,128,1536]{2,1,0:T(8,128)(2,1)}, bf16[2,128,1536]{2,1,0:T(8,128)(2,1)S(1)}, u32[]{:S(2)}) copy-start(bf16[2,128,1536]{2,1,0:T(8,128)(2,1)S(1)} %add_convert_fusion) | copy-start | bytes 2359300
  26.6 13.7 %collective-permute-start = (bf16[2,1,1536]{2,1,0:T(2,128)(2,1)S(1)}, bf16[2,1,1536]{2,1,0:T(2,128)(2,1)S(1)}, u32[]{:S(2)}, u32[]{:S(2)}) collective-permute-start(bf16[2,1,1536]{2,1,0:T(2,128)(2,1)S(1)} %get-tuple-element.40), channel_id=1, source_target_pairs={{0,8},{8,16},{16,24},{24,32},{32,40},{40,48},{48,56},{56,64},{64,7... | collective-permute-start | bytes 18440 | tf_op jit(solution)/shard_map/ppermute | solution.py:17
  28.5 7.7 %copy-start.2 = (bf16[2,128,1536]{2,1,0:T(8,128)(2,1)S(1)}, bf16[2,128,1536]{2,1,0:T(8,128)(2,1)}, u32[]{:S(2)}) copy-start(bf16[2,128,1536]{2,1,0:T(8,128)(2,1)} %custom-call) | copy-start | bytes 2359300
  28.5 12.4 %collective-permute-start.1 = (bf16[2,1,1536]{2,1,0:T(2,128)(2,1)S(1)}, bf16[2,1,1536]{2,1,0:T(2,128)(2,1)S(1)}, u32[]{:S(2)}, u32[]{:S(2)}) collective-permute-start(bf16[2,1,1536]{2,1,0:T(2,128)(2,1)S(1)} %get-tuple-element.41), channel_id=1, source_target_pairs={{8,0},{16,8},{24,16},{32,24},{40,32},{48,40},{56,48},{64,56},{72,6... | collective-permute-start | bytes 18440 | tf_op jit(solution)/shard_map/ppermute | solution.py:18
  36.2 43.5 %copy-start.1 = (bf16[2,128,1536]{2,1,0:T(8,128)(2,1)S(1)}, bf16[2,128,1536]{2,1,0:T(8,128)(2,1)}, u32[]{:S(2)}) copy-start(bf16[2,128,1536]{2,1,0:T(8,128)(2,1)} %copy-done) | copy-start | bytes 2359300
  40.3 51.6 %copy-start.3 = (bf16[2,128,1536]{2,1,0:T(8,128)(2,1)}, bf16[2,128,1536]{2,1,0:T(8,128)(2,1)S(1)}, u32[]{:S(2)}) copy-start(bf16[2,128,1536]{2,1,0:T(8,128)(2,1)S(1)} %get-tuple-element.11) | copy-start | bytes 2359300
  79.7 12.1 %copy-start.7 = (bf16[1536,1536]{1,0:T(8,128)(2,1)S(1)}, bf16[1536,1536]{1,0:T(8,128)(2,1)}, u32[]{:S(2)}) copy-start(bf16[1536,1536]{1,0:T(8,128)(2,1)} %all-gather.2.cloned.1.call-done) | copy-start | bytes 14155780
  88.0 128.8 %collective-permute-start.2 = (bf16[2,128,1536]{2,1,0:T(8,128)(2,1)}, bf16[2,128,1536]{2,1,0:T(8,128)(2,1)}, u32[]{:S(2)}, u32[]{:S(2)}) collective-permute-start(bf16[2,128,1536]{2,1,0:T(8,128)(2,1)} %fusion.10), channel_id=1, source_target_pairs={{8,0},{16,8},{24,16},{32,24},{40,32},{48,40},{56,48},{64,56},{72,6... | collective-permute-start | bytes 2359304 | tf_op jit(solution)/shard_map/ppermute | solution.py:26
  200.8 5.1 %collective-permute-start.4 = (bf16[2,1,1536]{2,1,0:T(2,128)(2,1)S(1)}, bf16[2,1,1536]{2,1,0:T(2,128)(2,1)S(1)}, u32[]{:S(2)}, u32[]{:S(2)}) collective-permute-start(bf16[2,1,1536]{2,1,0:T(2,128)(2,1)S(1)} %get-tuple-element.38), channel_id=1, source_target_pairs={{8,0},{16,8},{24,16},{32,24},{40,32},{48,40},{56,48},{64,56},{72,6... | collective-permute-start | bytes 18440 | tf_op jit(solution)/shard_map/ppermute | solution.py:18
  203.0 7.4 %collective-permute-start.5 = (bf16[2,1,1536]{2,1,0:T(2,128)(2,1)S(1)}, bf16[2,1,1536]{2,1,0:T(2,128)(2,1)S(1)}, u32[]{:S(2)}, u32[]{:S(2)}) collective-permute-start(bf16[2,1,1536]{2,1,0:T(2,128)(2,1)S(1)} %get-tuple-element.39), channel_id=1, source_target_pairs={{0,8},{8,16},{16,24},{24,32},{32,40},{40,48},{48,56},{56,64},{64,7... | collective-permute-start | bytes 18440 | tf_op jit(solution)/shard_map/ppermute | solution.py:17
Sparse Core Ops, SparseCore 0:
  10.1 69.5 all-gather.1
where the time goes:
time: 227 us; the launch traced here: 226 us
  blocking collectives  106 us (47%)
  waiting for transfers between devices  52 us (23%)
  starting transfers between devices  23.8 us (10%)
  between operations  14.3 us (6%)
  matrix products  13.5 us (6%)
  other arithmetic  9.01 us (4%)
  local copies, waits for them, and re-layouts  7.43 us (3%)
    psum x1, blocking collectives, shards(): filter_sum = lax.psum(filter_terms, ('seq', 'head'))  106 us
    all_gather x1, waiting for transfers between devices, shards(): full_weight = lax.all_gather(point_weight, 'head', axis=0, tiled=True)  38.8 us
    ppermute x2, starting transfers between devices, extended(): after = lax.ppermute(initial, axis, down)  8.39 us
    dot_general x1, matrix products, shards(): jnp.dot(flat_act, full_weight, preferred_element_type=jnp.float32)  8.3 us
    all_to_all x1, waiting for transfers between devices, shards(): lax.all_to_all(attention, 'head', split_axis=0, concat_axis=2, tiled=True)  7.36 us
    ppermute x2, starting transfers between devices, passed_along(): return lax.ppermute(shard, axis, pairs)  5.71 us
    all_to_all x1, starting transfers between devices, shards(): lax.all_to_all(attention, 'head', split_axis=0, concat_axis=2, tiled=True)  5.41 us
  transfers between devices with their start and end apart: 8, of which 4 were waited for; matrix products, arithmetic and copies ran while one was open for 9% of the time, Pallas kernels for 0%

commit v1 on v0

--- a/solution.py
+++ b/solution.py
@@ -46,6 +46,11 @@
 def shards(
     attention, encoder_skip, depth_filter, point_weight, crop_offset, target_bins, cotangent
 ):
+
+    def map_records_now(z_in, along_axis):
+        k_now = lax.all_gather(z_in, along_axis)
+        return jnp.sum(k_now, axis=0)
+
     slab_input = lax.all_to_all(attention, "head", split_axis=0, concat_axis=2, tiled=True)
     local_seqs = encoder_skip.shape[0]
     slab_rows = encoder_skip.shape[1]
@@ -122,7 +127,7 @@
             ),
         ]
     )
-    filter_sum = lax.psum(filter_terms, ("seq", "head"))
+    filter_sum = map_records_now(filter_terms, ("seq", "head"))
     row_count = local_seqs * lax.axis_size("head") * slab_rows * lax.axis_size("seq")
     filter_grad = filter_sum * (1.0 / math.sqrt(row_count))
     return (target_rows, attention_grad, skip_grad, filter_grad)

time: 227 us -> 1530 us (6.74)
  the two profiles are of different devices: /device:TPU:32 before, /device:TPU:99 now
where the time goes in v1:
time: 1530 us
  waiting for transfers between devices  1440 us (94%)
  starting transfers between devices  35 us (2%)
  matrix products  15.5 us (1%)
    all_gather x1, waiting for transfers between devices, map_records_now(): k_now = lax.all_gather(z_in, along_axis)  1400 us
    all_gather x1, waiting for transfers between devices, shards(): full_weight = lax.all_gather(point_weight, 'head', axis=0, tiled=True)  32.2 us
  transfers between devices with their start and end apart: 9, of which 4 were waited for; matrix products, arithmetic and copies ran while one was open for 2% of the time, Pallas kernels for 0%

profile of v1, /device:TPU:99, one launch (start us, length us, event | category | flops | bytes accessed | tf_op | source)
XLA Modules:
  0.0 1532.1 jit_solution(2848588407416943695)
XLA Ops:
  7.2 0.0 copy-start.7
  7.2 0.0 copy-start.5
  7.2 0.0 all-gather.5.cloned.1.call-start
  7.2 0.7 all-gather.5.cloned.1.call-update
  7.9 5.4 all-to-all-start
  13.3 0.0 all-gather.7.cloned.1.call-start
  13.3 4.9 collective-permute-start.3
  18.2 0.0 copy-done.7
  18.2 0.1 copy.15
  18.3 0.0 copy-done.5
  18.3 0.1 slice_reduce_fusion.2
  18.4 2.6 all-to-all-done
  21.0 0.3 copy.38
  21.3 0.3 reshape.54
  21.6 0.5 broadcast_in_dim.4
  22.2 1.1 convert_element_type.67
  23.3 1.3 add_convert_fusion
  24.6 0.0 copy-start
  24.6 4.1 collective-permute-start.1
  28.7 0.0 copy-start.2
  28.7 11.5 collective-permute-start
  40.3 0.0 copy-done
  40.3 0.0 collective-permute-done.3
  40.3 1.5 pad_maximum_fusion
  41.8 0.0 copy-done.2
  41.8 0.0 copy-start.1
  41.8 4.0 while.1
  41.8 0.6 fusion.117
  42.4 1.4 dynamic-slice_dynamic-update-slice_fusion.2
  43.8 0.6 fusion.117
  44.4 1.4 dynamic-slice_dynamic-update-slice_fusion.2
  45.8 0.0 copy-start.3
  45.9 0.0 collective-permute-done.1
  45.9 0.0 collective-permute-done
  45.9 32.2 %all-gather.5.cloned.1.call-done = bf16[1536,1536]{1,0:T(8,128)(2,1)} async-done(((bf16[192,1536]{1,0:T(8,128)(2,1)}), bf16[1536,1536]{1,0:T(8,128)(2,1)}) %all-gather.5.cloned.1.call-update) | async-done | bytes 4718608 | tf_op jit(solution)/shard_map/all_gather | solution.py:69
  78.0 0.0 copy-done.1
  78.0 4.9 fusion.25
  82.9 0.0 copy-done.3
  83.0 0.6 maximum_bitcast_fusion
  83.6 0.0 all-gather.7.cloned.1.call-update
  83.6 0.0 copy-start.6
  83.7 0.0 copy-start.4
  83.7 8.3 fusion.10
  91.9 2.6 collective-permute-start.2
  94.5 4.5 collective-permute-start.5
  99.0 2.1 collective-permute-start.4
  101.1 0.0 copy-done.6
  101.1 0.1 dynamic-slice_add_fusion
  101.2 0.0 collective-permute-done.5
  101.2 6.3 collective-permute-done.4
  107.5 0.0 copy-done.4
  107.5 1.5 fusion.111
  109.0 0.9 reshape.30
  110.0 2.8 reduce_sum.18
  112.8 0.0 collective-permute-done.2
  112.8 2.3 convolution_convert_fusion
  115.1 1403.2 %all-gather.7.cloned.1.call-done = f32[512,3,1536]{2,1,0:T(4,128)} async-done(((f32[1,3,1536]{2,1,0:T(4,128)}), f32[512,3,1536]{2,1,0:T(4,128)}) %all-gather.7.cloned.1.call-update) | async-done | bytes 9437200 | tf_op jit(solution)/shard_map/all_gather | solution.py:51
  1518.4 6.3 reduce_sum.19
  1524.7 0.6 broadcast_multiply_fusion
  (11 shorter events, 0.1 us)
Async XLA Ops:
  7.2 11.0 copy-start.7
  7.2 11.2 copy-start.5
  7.2 70.9 %all-gather.5.cloned.1.call-start = ((), (), s32[]{:S(2)}) async-start(), calls=%async_computation.1 | async-start | bytes 5308416 | tf_op jit(solution)/shard_map/all_gather | solution.py:69
  7.9 13.1 all-to-all-start
  13.3 1505.1 %all-gather.7.cloned.1.call-start = ((), (), s32[]{:S(2)}) async-start(), calls=%async_computation.2 | async-start | bytes 12607488 | tf_op jit(solution)/shard_map/all_gather | solution.py:51
  13.3 27.0 %collective-permute-start.3 = (bf16[2,128,1536]{2,1,0:T(8,128)(2,1)}, bf16[2,128,1536]{2,1,0:T(8,128)(2,1)}, u32[]{:S(2)}, u32[]{:S(2)}) collective-permute-start(bf16[2,128,1536]{2,1,0:T(8,128)(2,1)} %param.13), channel_id=1, source_target_pairs={{0,8},{8,16},{16,24},{24,32},{32,40},{40,48},{48,56},{56,64},{64,7... | collective-permute-start | bytes 2359304 | tf_op jit(solution)/shard_map/ppermute | solution.py:26
  24.6 15.7 %copy-start = (bf16[2,128,1536]{2,1,0:T(8,128)(2,1)}, bf16[2,128,1536]{2,1,0:T(8,128)(2,1)S(1)}, u32[]{:S(2)}) copy-start(bf16[2,128,1536]{2,1,0:T(8,128)(2,1)S(1)} %add_convert_fusion) | copy-start | bytes 2359300
  24.6 21.2 %collective-permute-start.1 = (bf16[2,1,1536]{2,1,0:T(2,128)(2,1)S(1)}, bf16[2,1,1536]{2,1,0:T(2,128)(2,1)S(1)}, u32[]{:S(2)}, u32[]{:S(2)}) collective-permute-start(bf16[2,1,1536]{2,1,0:T(2,128)(2,1)S(1)} %get-tuple-element.45), channel_id=1, source_target_pairs={{8,0},{16,8},{24,16},{32,24},{40,32},{48,40},{56,48},{64,56},{72,6... | collective-permute-start | bytes 18440 | tf_op jit(solution)/shard_map/ppermute | solution.py:18
  28.7 13.0 copy-start.2
  28.7 17.1 %collective-permute-start = (bf16[2,1,1536]{2,1,0:T(2,128)(2,1)S(1)}, bf16[2,1,1536]{2,1,0:T(2,128)(2,1)S(1)}, u32[]{:S(2)}, u32[]{:S(2)}) collective-permute-start(bf16[2,1,1536]{2,1,0:T(2,128)(2,1)S(1)} %get-tuple-element.44), channel_id=1, source_target_pairs={{0,8},{8,16},{16,24},{24,32},{32,40},{40,48},{48,56},{56,64},{64,7... | collective-permute-start | bytes 18440 | tf_op jit(solution)/shard_map/ppermute | solution.py:17
  41.8 36.2 %copy-start.1 = (bf16[2,128,1536]{2,1,0:T(8,128)(2,1)S(1)}, bf16[2,128,1536]{2,1,0:T(8,128)(2,1)}, u32[]{:S(2)}) copy-start(bf16[2,128,1536]{2,1,0:T(8,128)(2,1)} %copy-done) | copy-start | bytes 2359300
  45.8 37.1 %copy-start.3 = (bf16[2,128,1536]{2,1,0:T(8,128)(2,1)}, bf16[2,128,1536]{2,1,0:T(8,128)(2,1)S(1)}, u32[]{:S(2)}) copy-start(bf16[2,128,1536]{2,1,0:T(8,128)(2,1)S(1)} %get-tuple-element.11) | copy-start | bytes 2359300
  83.6 17.5 %copy-start.6 = (s32[2,128]{1,0:T(2,128)S(1)}, s32[2,128]{1,0:T(2,128)}, u32[]{:S(2)}) copy-start(s32[2,128]{1,0:T(2,128)} %param.12) | copy-start | bytes 3076
  83.7 23.8 %copy-start.4 = (bf16[2,128,1536]{2,1,0:T(8,128)(2,1)S(1)}, bf16[2,128,1536]{2,1,0:T(8,128)(2,1)}, u32[]{:S(2)}) copy-start(bf16[2,128,1536]{2,1,0:T(8,128)(2,1)} %copy-done.3) | copy-start | bytes 2359300
  91.9 20.9 %collective-permute-start.2 = (bf16[2,128,1536]{2,1,0:T(8,128)(2,1)}, bf16[2,128,1536]{2,1,0:T(8,128)(2,1)}, u32[]{:S(2)}, u32[]{:S(2)}) collective-permute-start(bf16[2,128,1536]{2,1,0:T(8,128)(2,1)} %fusion.10), channel_id=1, source_target_pairs={{8,0},{16,8},{24,16},{32,24},{40,32},{48,40},{56,48},{64,56},{72,6... | collective-permute-start | bytes 2359304 | tf_op jit(solution)/shard_map/ppermute | solution.py:26
  94.5 6.7 collective-permute-start.5
  99.0 8.5 collective-permute-start.4
Sparse Core Ops, SparseCore 0:
  10.1 67.8 all-gather.4
  83.8 1434.5 all-gather.6
